TPU v7x, 32 devices: a whole 2x2x4 slice. The times are simulated.
32 devices in a mesh: site: 2 (over y), pts: 4 (over z), var: 2 (over x), cmp: 2 (over core).
Axes of the slice: x: 2, y: 2, z: 4, core: 2. Of those that a mesh axis runs over, the one named last changes fastest.
Arguments:
- sgt: bfloat16 [6, 3, 128, 4096], P('cmp', None, ('site', 'pts')), parts along dimension 2, may hold values from -6 to 6
- moment: float32 [6, 64], P('cmp', ('site', 'pts')), parts along dimension 1, may hold values from -6 to 6
- slip_spec: float32 [16, 2, 4096], replicated, may hold values from -3 to 3
- rp_slab: int32 [64], P('site'), parts along dimension 0, may hold values from 0 to 63, as said below
- rup_counts: int32 [8, 6], P(('site', 'pts')), parts along dimension 0, may hold values from 1 to 2, 8 in all within a row
- var_rupture: int32 [32], P('site'), parts along dimension 0, may hold values from 0 to 5
- var_source: int32 [32, 2], P('site'), parts along dimension 0, may hold values from 0 to 15
- owner_map: int32 [32], P('site'), parts along dimension 0, may hold values from 0 to 15, each once
Outputs:
- seismograms: float32 [32, 3, 4096], P(('site', 'pts', 'var', 'cmp')), parts along dimension 0
There are 2 independent parts, one for each index of `site`. A program takes and returns all parts, laid end to end along the dimension named above; an argument that names none is the same for every part. Nothing has to cross between parts.
Inputs may be any that keep to these rules, and one draw needn't show every extreme that they name: `rp_slab`: in each aligned block of 8 rupture-points (one owner's), at most 4 name slab points of one reader (slab points k * 16 to (k + 1) * 16 - 1 belong to reader k), and in every block some reader is named exactly 4 times. `rup_counts`: each row gives, for the ruptures in order, how many of that owner's 8 slots belong to each; every rupture has 1 or more on every owner, the row sums to 8, and some entry of each row is exactly 2. `owner_map`: A permutation of the variations.
All inputs are finite; a program needn't handle non-finite values.
Results may differ from a plain program's by a relative error of at most 0.0003.
Values may be sent and summed in bfloat16 or wider, within the bound.
No kernel may reach another device: no remote copies, remote signals or barrier semaphores. Data moves between devices by JAX's collectives and lax.ppermute only.
A program may use at most 64 MiB of HBM per device.

v0:
```python
import math
import jax
import jax.numpy as jnp
from jax import lax
from jax.sharding import PartitionSpec as P

TAU = 4
highest = lax.Precision.HIGHEST


def cos_sin(numerator, period):
    angles = numerator.astype(jnp.float32) * (2.0 * math.pi / period)
    return (jnp.cos(angles), jnp.sin(angles))


def forward_spectra(signal):
    series, samples = signal.shape
    length = 2 * samples
    blocks = length // 128
    rows_half = blocks // 2
    row_iota = jnp.arange(rows_half, dtype=jnp.int32)
    outer_iota = jnp.arange(blocks, dtype=jnp.int32)
    lane_iota = jnp.arange(128, dtype=jnp.int32)
    half_iota = jnp.arange(64, dtype=jnp.int32)
    first_cos, first_sin = cos_sin(row_iota[:, None] * outer_iota[None, :] % blocks, blocks)
    first_table = jnp.concatenate([first_cos, -first_sin], axis=1)
    shaped = signal.reshape(series, rows_half, 128)
    first_pass = jnp.einsum("sab,am->smb", shaped, first_table, precision=highest)
    real_part = first_pass[:, :blocks]
    imag_part = first_pass[:, blocks:]
    turn_cos, turn_sin = cos_sin(outer_iota[:, None] * lane_iota[None, :], length)
    turned_real = real_part * turn_cos + imag_part * turn_sin
    turned_imag = imag_part * turn_cos - real_part * turn_sin
    second_cos, second_sin = cos_sin(lane_iota[:, None] * half_iota[None, :] % 128, 128)
    second_table = jnp.concatenate(
        [
            jnp.concatenate([second_cos, -second_sin], axis=1),
            jnp.concatenate([second_sin, second_cos], axis=1),
        ],
        axis=0,
    )
    joined = jnp.concatenate([turned_real, turned_imag], axis=-1)
    return jnp.einsum("skb,bm->skm", joined, second_table, precision=highest)


def inverse_series(spectra):
    series, blocks, lanes = spectra.shape
    samples = blocks * 64
    length = 2 * samples
    rows_half = blocks // 2
    outer_iota = jnp.arange(blocks, dtype=jnp.int32)
    lane_iota = jnp.arange(128, dtype=jnp.int32)
    half_iota = jnp.arange(64, dtype=jnp.int32)
    row_iota = jnp.arange(rows_half, dtype=jnp.int32)
    frequency = outer_iota[:, None] + blocks * half_iota[None, :]
    weights = jnp.where(frequency == 0, 1.0, 2.0).astype(jnp.float32) / length
    weights = jnp.concatenate([weights, weights], axis=-1)
    scaled = spectra * weights[None]
    third_cos, third_sin = cos_sin(half_iota[:, None] * lane_iota[None, :] % 128, 128)
    third_table = jnp.concatenate(
        [
            jnp.concatenate([third_cos, third_sin], axis=1),
            jnp.concatenate([-third_sin, third_cos], axis=1),
        ],
        axis=0,
    )
    middle = jnp.einsum("skm,mb->skb", scaled, third_table, precision=highest)
    mid_real = middle[..., :128]
    mid_imag = middle[..., 128:]
    turn_cos, turn_sin = cos_sin(outer_iota[:, None] * lane_iota[None, :], length)
    back_real = mid_real * turn_cos - mid_imag * turn_sin
    back_imag = mid_real * turn_sin + mid_imag * turn_cos
    stacked = jnp.concatenate([back_real, back_imag], axis=1)
    last_cos, last_sin = cos_sin(outer_iota[:, None] * row_iota[None, :] % blocks, blocks)
    last_table = jnp.concatenate([last_cos, -last_sin], axis=0)
    result = jnp.einsum("smb,ma->sab", stacked, last_table, precision=highest)
    return result.reshape(series, samples)


def per_device(sgt, moment, slip_spec, rp_slab, rup_counts, var_rupture, var_source, owner_map):
    comp_half, seis_comp, slab_dev, samples = sgt.shape
    rp_dev = moment.shape[1]
    owners = lax.axis_size("pts")
    my_owner = lax.axis_index("pts")
    var_count = lax.axis_size("var")
    my_var = lax.axis_index("var")
    cmp_count = lax.axis_size("cmp")
    my_core = lax.axis_index("cmp")
    capacity = max(2, (2 * rp_dev + owners - 1) // owners)
    length = 2 * samples
    blocks = length // 128
    readers = rp_slab // slab_dev
    within = rp_slab % slab_dev
    reader_rows = readers.reshape(owners, rp_dev)
    slot_iota = jnp.arange(rp_dev, dtype=jnp.int32)
    lower_slot = slot_iota[None, :] < slot_iota[:, None]
    same_reader = reader_rows[:, :, None] == reader_rows[:, None, :]
    ranks = jnp.sum(same_reader & lower_slot[None], axis=2)
    owner_ids = jnp.arange(owners, dtype=jnp.int32)[:, None]
    target = (owner_ids * capacity + ranks).reshape(-1)
    spill = owners * capacity
    place = jnp.where(readers == my_owner, target, spill)
    send_rows = jnp.zeros((spill,), jnp.int32).at[place].set(within, mode="drop")
    send_live = jnp.zeros((spill,), jnp.bool_).at[place].set(True, mode="drop")
    outgoing = jnp.take(sgt, send_rows, axis=2)
    outgoing = jnp.where(send_live[None, None, :, None], outgoing, jnp.zeros((), outgoing.dtype))
    received = lax.all_to_all(outgoing, "pts", split_axis=2, concat_axis=2, tiled=True)
    pick_rows = reader_rows[my_owner] * capacity + ranks[my_owner]
    picked = jnp.take(received, pick_rows, axis=2)
    partial_value = jnp.sum(moment[:, None, :, None] * picked.astype(jnp.float32), axis=0)
    pieces = lax.all_to_all(partial_value[None], "cmp", split_axis=2, concat_axis=0, tiled=True)
    half_sum = jnp.sum(pieces, axis=0)
    half_points = rp_dev // cmp_count
    half_spec = forward_spectra(half_sum.reshape(seis_comp * half_points, samples)).reshape(
        seis_comp, half_points, blocks, 128
    )
    spectra = lax.all_gather(half_spec, "cmp", axis=1, tiled=True)
    counts_all = lax.all_gather(rup_counts, "pts", axis=0, tiled=True)
    my_counts = rup_counts[0]
    ruptures = my_counts.shape[0]
    rupture_iota = jnp.arange(ruptures, dtype=jnp.int32)
    inclusive = jnp.cumsum(my_counts)
    rupture_of = jnp.sum(inclusive[None, :] <= slot_iota[:, None], axis=1)
    owner_mask = (jnp.arange(owners, dtype=jnp.int32) < my_owner)[:, None]
    before = jnp.sum(jnp.where(owner_mask, counts_all, 0), axis=0)
    lengths = jnp.sum(counts_all, axis=0)
    point_onehot = (rupture_of[:, None] == rupture_iota[None, :]).astype(jnp.int32)
    shift_table = before - inclusive + my_counts
    position = slot_iota + jnp.sum(point_onehot * shift_table[None, :], axis=1)
    outer_iota = jnp.arange(blocks, dtype=jnp.int32)
    half_iota = jnp.arange(64, dtype=jnp.int32)
    frequency = outer_iota[:, None] + blocks * half_iota[None, :]
    point_cos, point_sin = cos_sin(
        frequency[None] * (TAU * position)[:, None, None] % length, length
    )
    point_cos = point_cos[None]
    point_sin = point_sin[None]
    real_x = spectra[..., :64]
    imag_x = spectra[..., 64:]
    lagged = jnp.concatenate(
        [real_x * point_cos + imag_x * point_sin, imag_x * point_cos - real_x * point_sin], axis=-1
    )
    leading = jnp.concatenate(
        [real_x * point_cos - imag_x * point_sin, imag_x * point_cos + real_x * point_sin], axis=-1
    )
    per_owner = owner_map.shape[0] // (owners * var_count * cmp_count)
    row_owner = jnp.arange(owners, dtype=jnp.int32)[:, None]
    row_unit = jnp.arange(per_owner, dtype=jnp.int32)[None, :]
    slot_ids = (
        ((row_owner * var_count + my_var) * cmp_count + my_core) * per_owner + row_unit
    ).reshape(-1)
    var_ids = owner_map[slot_ids]
    var_rup = var_rupture[var_ids]
    hypo_index = var_source[var_ids, 0]
    slip_index = var_source[var_ids, 1]
    functions = slip_spec.shape[0]
    rup_onehot = (var_rup[:, None] == rupture_iota[None, :]).astype(jnp.int32)
    rup_length = jnp.sum(rup_onehot * lengths[None, :], axis=1)
    hypocenter = hypo_index * rup_length // functions
    same_rup = var_rup[:, None] == rupture_of[None, :]
    ahead_mask = (same_rup & (position[None, :] >= hypocenter[:, None])).astype(jnp.float32)
    behind_mask = (same_rup & (position[None, :] < hypocenter[:, None])).astype(jnp.float32)
    hypo_cos, hypo_sin = cos_sin(
        frequency[None] * (TAU * hypocenter)[:, None, None] % length, length
    )
    slip_rows = slip_spec[slip_index].reshape(slip_index.shape[0], 2, 64, blocks)
    slip_rows = jnp.transpose(slip_rows, (0, 3, 1, 2)).reshape(slip_index.shape[0], blocks, 128)
    first_sum = jnp.einsum("vq,cqkm->vckm", ahead_mask, lagged, precision=highest)
    second_sum = jnp.einsum("vq,cqkm->vckm", behind_mask, leading, precision=highest)
    rows_cos = hypo_cos[:, None]
    rows_sin = hypo_sin[:, None]
    rows_slip = slip_rows[:, None]
    sum_real = first_sum[..., :64] + second_sum[..., :64]
    diff_real = first_sum[..., :64] - second_sum[..., :64]
    sum_imag = first_sum[..., 64:] + second_sum[..., 64:]
    diff_imag = first_sum[..., 64:] - second_sum[..., 64:]
    turned_real = rows_cos * sum_real - rows_sin * diff_imag
    turned_imag = rows_cos * sum_imag + rows_sin * diff_real
    slip_real = rows_slip[..., :64]
    slip_imag = rows_slip[..., 64:]
    totals = lax.psum_scatter(
        jnp.concatenate(
            [
                slip_real * turned_real - slip_imag * turned_imag,
                slip_real * turned_imag + slip_imag * turned_real,
            ],
            axis=-1,
        ),
        "pts",
        scatter_dimension=0,
        tiled=True,
    )
    result = inverse_series(totals.reshape(per_owner * seis_comp, blocks, 128)).reshape(
        per_owner, seis_comp, samples
    )
    return result


def solution(mesh):
    placed = (
        P("cmp", None, ("site", "pts"), None),
        P("cmp", ("site", "pts")),
        P(),
        P("site"),
        P(("site", "pts"), None),
        P("site"),
        P("site", None),
        P("site"),
    )
    return jax.shard_map(
        per_device,
        mesh=mesh,
        in_specs=placed,
        out_specs=P(("site", "pts", "var", "cmp"), None, None),
        check_vma=False,
    )
```

profile of v0, /device:TPU:0, one launch (start us, length us, event | category | flops | bytes accessed | tf_op | source)
XLA Modules:
  0.0 121.4 jit_solution(11977667582550914608)
XLA Ops:
  6.6 0.8 and_select_fusion
  7.4 0.2 convert_reduce_fusion
  7.8 0.7 scatter_custom_fusion.1
  8.5 3.9 %gather_fusion.5 = bf16[16,3,3,4096]{3,0,2,1:T(8,128)(2,1)S(1)} fusion(bf16[3,3,16,4096]{3,2,1,0:T(8,128)(2,1)S(1)} %copy-done, s32[1024]{0:T(1024)S(1)} %pad_clamp_fusion.1), kind=kCustom, calls=%fused_computation.5 | custom fusion | bytes 2359360 | tf_op jit(solution)/shard_map/jit(_take)/gather | solution.py:105
  12.5 0.7 scatter_custom_fusion
  13.1 0.2 select_bitcast_fusion
  13.3 2.2 %copy.52 = bf16[3,3,16,4096]{3,1,0,2:T(4,128)(2,1)} copy(bf16[3,3,16,4096]{3,2,1,0:T(8,128)(2,1)S(1)} %select_bitcast_fusion) | data formatting | bytes 2359296 | tf_op jit(solution)/shard_map/jit(_where)/select_n | solution.py:106
  15.5 6.5 %all-to-all-start = ((bf16[3,3,16,4096]{3,1,0,2:T(4,128)(2,1)}), bf16[3,3,16,4096]{3,1,0,2:T(4,128)(2,1)S(1)}, u32[]{:S(2)}, u32[]{:S(2)}) async-start(bf16[3,3,16,4096]{3,1,0,2:T(4,128)(2,1)} %copy.52), calls=%async_computation | async-start | bytes 3145728 | tf_op jit(solution)/shard_map/all_to_all | solution.py:107
  22.0 0.7 sine_negate_fusion
  22.7 0.5 compare_and_fusion.3
  23.4 30.0 %all-gather = s32[4,1,6]{2,1,0:T(1,128)S(1)} all-gather(s32[1,1,6]{2,1,0:T(1,128)S(1)} %bitcast.102), channel_id=1, replica_groups=mesh['site'=2,'pts'=4,'var'=2,'cmp'=2] {'pts'}, dimensions={0}, use_global_device_ids=true | all-gather | bytes 120 | tf_op jit(solution)/shard_map/all_gather | solution.py:118
  53.4 0.2 reduce-window.4
  53.8 0.6 gather_fusion
  54.5 0.6 gather_fusion.3
  55.2 0.6 gather_fusion.1
  55.8 1.7 %gather_fusion.2 = f32[4,2,4096]{2,1,0:T(2,128)S(1)} fusion(f32[16,2,4096]{2,1,0:T(2,128)} %param.10, s32[1024]{0:T(1024)S(1)} %pad_clamp_fusion.3), kind=kCustom, calls=%fused_computation.2 | custom fusion | bytes 262160 | tf_op jit(solution)/shard_map/gather | solution.py:166
  57.6 0.2 reshape.311
  58.0 0.6 gather_fusion.4
  58.7 0.2 select_reduce_fusion
  58.9 0.2 select_reduce_fusion.2
  59.0 0.8 fusion.56
  59.8 0.9 fusion.61
  60.7 0.9 fusion.54
  61.6 0.5 iota_add_fusion.1
  62.2 1.9 %fusion.48 = (f32[4,64,64]{2,0,1:T(4,128)}, f32[4,64,64]{2,0,1:T(4,128)}) fusion(s32[4]{0:T(128)S(1)} %get-tuple-element.8, s32[64,64]{1,0:T(8,128)S(1)} %iota_add_fusion), kind=kLoop, calls=%fused_computation.89 | loop fusion | flops 229376 | bytes 147472 | tf_op jit(solution)/shard_map/cos | solution.py:13
  64.0 1.1 fusion.41
  65.1 1.8 %copy.53 = bf16[3,3,16,4096]{3,1,2,0:T(4,128)(2,1)} copy(bf16[3,3,16,4096]{3,1,0,2:T(4,128)(2,1)S(1)} %all-to-all-done) | data formatting | bytes 2359296 | tf_op jit(solution)/shard_map/all_to_all | solution.py:107
  67.0 2.6 %gather_fusion.6 = bf16[8,3,3,4096]{3,2,1,0:T(4,128)(2,1)S(1)} fusion(bf16[3,3,16,4096]{3,1,2,0:T(4,128)(2,1)} %copy.53, s32[1024]{0:T(1024)S(1)} %pad_clamp_fusion), kind=kCustom, calls=%fused_computation.6 | custom fusion | bytes 1179680 | tf_op jit(solution)/shard_map/jit(_take)/gather | solution.py:109
  69.6 0.7 fusion
  70.3 0.4 copy.54
  70.7 4.0 %all_to_all.17 = f32[1,3,8,4096]{3,0,1,2:T(1,128)S(1)} all-to-all(f32[1,3,8,4096]{3,0,1,2:T(1,128)S(1)} %copy.54), channel_id=1, replica_groups=mesh['site'=2,'pts'=4,'var'=2,'cmp'=2] {'cmp'}, dimensions={2} | all-to-all | bytes 786432 | tf_op jit(solution)/shard_map/all_to_all | solution.py:111
  74.8 0.3 copy.67
  75.1 0.2 reduce_sum.82
  75.6 0.9 convolution_bitcast_fusion
  76.7 0.9 fusion.1
  77.6 2.4 %all_gather.7 = f32[3,8,64,128]{3,2,0,1:T(8,128)S(1)} all-gather(f32[3,4,64,128]{3,2,0,1:T(8,128)S(1)} %copy.58), channel_id=1, replica_groups=mesh['site'=2,'pts'=4,'var'=2,'cmp'=2] {'cmp'}, dimensions={1}, use_global_device_ids=true | all-gather | bytes 1179648 | tf_op jit(solution)/shard_map/all_gather | solution.py:117
  79.9 0.3 fusion.114
  80.3 1.0 fusion.14
  81.3 0.6 fusion.5
  81.9 0.6 fusion.9
  82.6 0.3 copy-done.4
  82.9 0.5 multiply_subtract_fusion
  83.5 0.3 pad_maximum_fusion
  83.8 0.8 copy.61
  84.7 0.1 fusion.73
  85.0 27.4 %reduce-scatter.2.cloned.1.call-done = f32[1,3,64,128]{3,2,1,0:T(8,128)} async-done(((f32[4,3,64,128]{3,2,1,0:T(8,128)}), f32[1,3,64,128]{3,2,1,0:T(8,128)}) %reduce-scatter.2.cloned.1.call-update) | async-done | bytes 98320 | tf_op jit(solution)/shard_map/reduce_scatter | solution.py:181
  112.4 1.2 fusion.33
  113.6 0.9 fusion.20
  (83 shorter events, 1.8 us)
Async XLA Ops:
  6.5 2.0 %copy-start = (bf16[3,3,16,4096]{3,2,1,0:T(8,128)(2,1)S(1)}, bf16[3,3,16,4096]{3,2,1,0:T(8,128)(2,1)}, u32[]{:S(2)}) copy-start(bf16[3,3,16,4096]{3,2,1,0:T(8,128)(2,1)} %param.8) | copy-start | bytes 3538948
  15.5 7.8 %copy-start.19 = (f32[3,8]{1,0:T(4,128)S(1)}, f32[3,8]{1,0:T(4,128)}, u32[]{:S(2)}) copy-start(f32[3,8]{1,0:T(4,128)} %param.9) | copy-start | bytes 292
  15.5 7.9 %copy-start.20 = (s32[1,6]{1,0:T(1,128)S(1)}, s32[1,6]{1,0:T(1,128)}, u32[]{:S(2)}) copy-start(s32[1,6]{1,0:T(1,128)} %param.12) | copy-start | bytes 76
  15.5 38.3 %copy-start.2 = (s32[16]{0:T(128)S(1)}, s32[16]{0:T(128)}, u32[]{:S(2)}) copy-start(s32[16]{0:T(128)} %param.15) | copy-start | bytes 196
  15.5 39.0 %copy-start.1 = (s32[16,2]{0,1:T(2,128)S(1)}, s32[16,2]{0,1:T(2,128)}, u32[]{:S(2)}) copy-start(s32[16,2]{0,1:T(2,128)} %param.14) | copy-start | bytes 388
  15.5 49.6 %all-to-all-start = ((bf16[3,3,16,4096]{3,1,0,2:T(4,128)(2,1)}), bf16[3,3,16,4096]{3,1,0,2:T(4,128)(2,1)S(1)}, u32[]{:S(2)}, u32[]{:S(2)}) async-start(bf16[3,3,16,4096]{3,1,0,2:T(4,128)(2,1)} %copy.52), calls=%async_computation | async-start | bytes 3145728 | tf_op jit(solution)/shard_map/all_to_all | solution.py:107
  22.0 90.4 %reduce-scatter.2.cloned.1.call-start = ((), (), s32[]{:S(2)}) async-start(), calls=%async_computation.3 | async-start | bytes 491520 | tf_op jit(solution)/shard_map/reduce_scatter | solution.py:181
  53.8 4.9 %copy-start.13 = (s32[8]{0:T(128)}, s32[8]{0:T(128)S(1)}, u32[]{:S(2)}) copy-start(s32[8]{0:T(128)S(1)} %convert_reduce_fusion.1) | copy-start | bytes 100
  55.2 2.9 %copy-start.3 = (s32[16]{0:T(128)S(1)}, s32[16]{0:T(128)}, u32[]{:S(2)}) copy-start(s32[16]{0:T(128)} %param.13) | copy-start | bytes 196
  58.7 5.4 %copy-start.15 = (s32[64]{0:T(128)}, s32[64]{0:T(128)S(1)}, u32[]{:S(2)}) copy-start(s32[64]{0:T(128)S(1)} %iota_multiply_fusion.2) | copy-start | bytes 772
  67.0 2.6 %copy-start.18 = (pred[8]{0:T(512)(128)(4,1)S(1)}, pred[8]{0:T(512)(128)(4,1)}, u32[]{:S(2)}) copy-start(pred[8]{0:T(512)(128)(4,1)} %get-tuple-element.10) | copy-start | bytes 28
  74.8 0.8 copy-start.11
  74.8 0.8 copy-start.12
  75.1 1.4 %copy-start.6 = (f32[64,128]{1,0:T(8,128)S(1)}, f32[64,128]{1,0:T(8,128)}, u32[]{:S(2)}) copy-start(f32[64,128]{1,0:T(8,128)} %get-tuple-element.37) | copy-start | bytes 98308
  75.1 1.4 %copy-start.7 = (f32[64,128]{1,0:T(8,128)S(1)}, f32[64,128]{1,0:T(8,128)}, u32[]{:S(2)}) copy-start(f32[64,128]{1,0:T(8,128)} %get-tuple-element.38) | copy-start | bytes 98308
  75.6 1.1 copy-start.8
  75.6 1.1 copy-start.9
  75.6 1.1 copy-start.10
  80.2 1.0 copy-start.14
  80.2 1.0 copy-start.17
  81.9 0.9 copy-start.4
  81.9 1.0 copy-start.5
  83.5 1.3 %copy-start.16 = (s32[64]{0:T(128)S(1)}, s32[64]{0:T(128)}, u32[]{:S(2)}) copy-start(s32[64]{0:T(128)} %copy-done.15) | copy-start | bytes 772
Sparse Core Ops, SparseCore 0:
  84.7 27.6 reduce-scatter.1
where the time goes:
time: 122 us; the launch traced here: 121 us
  blocking collectives  36.4 us (30%)
  waiting for transfers between devices  27.4 us (22%)
  local copies, waits for them, and re-layouts  19.3 us (16%)
  between operations  13.9 us (11%)
  other arithmetic  12.7 us (10%)
  starting transfers between devices  6.49 us (5%)
  matrix products  5.1 us (4%)
    all_gather x1, blocking collectives, per_device(): counts_all = lax.all_gather(rup_counts, 'pts', axis=0, tiled=True)  30 us
    reduce_scatter x1, waiting for transfers between devices, per_device(): lax.psum_scatter(jnp.concatenate([slip_real * turned_real - slip_imag * t...  27.4 us
    all_to_all x1, starting transfers between devices, per_device(): lax.all_to_all(outgoing, 'pts', split_axis=2, concat_axis=2, tiled=True)  6.49 us
    all_to_all x1, blocking collectives, per_device(): lax.all_to_all(partial_value[None], 'cmp', split_axis=2, concat_axis=0, t...  4.05 us
    gather x1, local copies, waits for them, and re-layouts, per_device(): outgoing = jnp.take(sgt, send_rows, axis=2)  3.92 us
    cos x3, other arithmetic, cos_sin(): return (jnp.cos(angles), jnp.sin(angles))  3.1 us
    gather x1, local copies, waits for them, and re-layouts, per_device(): picked = jnp.take(received, pick_rows, axis=2)  2.62 us
  transfers between devices with their start and end apart: 2, of which 1 were waited for; matrix products, arithmetic and copies ran while one was open for 11% of the time, Pallas kernels for 0%

commit v1 on v0

--- a/solution.py
+++ b/solution.py
@@ -1,3 +1,4 @@
+import functools
 import math
 import jax
 import jax.numpy as jnp
@@ -6,6 +7,18 @@
 
 TAU = 4
 highest = lax.Precision.HIGHEST
+
+
+def signs_number(mine_x, lane_axis):
+    o_now = lax.axis_size(lane_axis)
+    moved = jnp.split(mine_x, o_now, axis=2)
+    now = jnp.stack(moved)
+    newest = lax.all_to_all(now, lane_axis, 0, 0)
+    r2 = jnp.concatenate(newest, axis=2)
+    return r2
+
+
+frames_lead = functools.partial(signs_number, lane_axis="pts")
 
 
 def cos_sin(numerator, period):
@@ -104,7 +117,7 @@
     send_live = jnp.zeros((spill,), jnp.bool_).at[place].set(True, mode="drop")
     outgoing = jnp.take(sgt, send_rows, axis=2)
     outgoing = jnp.where(send_live[None, None, :, None], outgoing, jnp.zeros((), outgoing.dtype))
-    received = lax.all_to_all(outgoing, "pts", split_axis=2, concat_axis=2, tiled=True)
+    received = frames_lead(outgoing)
     pick_rows = reader_rows[my_owner] * capacity + ranks[my_owner]
     picked = jnp.take(received, pick_rows, axis=2)
     partial_value = jnp.sum(moment[:, None, :, None] * picked.astype(jnp.float32), axis=0)

time: 122 us -> 114 us (0.934)
  blocking collectives: 36.4 us -> 29.1 us
  waiting for transfers between devices: 27.4 us -> 25.3 us
  other arithmetic: 12.7 us -> 14.2 us
    all_gather x1, blocking collectives: 30 us -> 22.5 us  [per_device(): counts_all = lax.all_gather(rup_counts, 'pts', axis=0, tiled=True)]
    reshape x0 -> x1, local copies, waits for them, and re-layouts: none -> 2.61 us  [signs_number(): r2 = jnp.concatenate(newest, axis=2)]
    select_n x1 -> x0, local copies, waits for them, and re-layouts: 2.17 us -> none  [per_device(): jnp.where(send_live[None, None, :, None], outgoing, jnp.zeros((), outgoin...]
    reduce_scatter x1, waiting for transfers between devices: 27.4 us -> 25.3 us  [per_device(): lax.psum_scatter(jnp.concatenate([slip_real * turned_real - slip_imag * t...]
    another operation x1 -> x2, other arithmetic: 0.18 us -> 2.29 us  [the longest x1 2.11 us: signs_number(): now = jnp.stack(moved)]
    all_to_all x1 -> x0, local copies, waits for them, and re-layouts: 1.83 us -> none  [per_device(): lax.all_to_all(outgoing, 'pts', split_axis=2, concat_axis=2, tiled=True)]
  transfers between devices with their start and end apart: 2 -> 2, of which waited for: 1 -> 1; matrix products, arithmetic and copies ran while one was open for 11% -> 12% of each run, Pallas kernels for 0% -> 0%
where the time goes in v1:
time: 114 us; the launch traced here: 113 us
  blocking collectives  29.1 us (26%)
  waiting for transfers between devices  25.3 us (22%)
  local copies, waits for them, and re-layouts  19.2 us (17%)
  other arithmetic  14.2 us (12%)
  between operations  13.9 us (12%)
  starting transfers between devices  6.49 us (6%)
  matrix products  5.1 us (4%)
    reduce_scatter x1, waiting for transfers between devices, per_device(): lax.psum_scatter(jnp.concatenate([slip_real * turned_real - slip_imag * t...  25.3 us
    all_gather x1, blocking collectives, per_device(): counts_all = lax.all_gather(rup_counts, 'pts', axis=0, tiled=True)  22.5 us
    all_to_all x1, starting transfers between devices, signs_number(): newest = lax.all_to_all(now, lane_axis, 0, 0)  6.49 us
    all_to_all x1, blocking collectives, per_device(): lax.all_to_all(partial_value[None], 'cmp', split_axis=2, concat_axis=0, t...  4.05 us
    gather x1, local copies, waits for them, and re-layouts, per_device(): outgoing = jnp.take(sgt, send_rows, axis=2)  3.92 us
    gather x1, local copies, waits for them, and re-layouts, per_device(): picked = jnp.take(received, pick_rows, axis=2)  2.75 us
    reshape x1, local copies, waits for them, and re-layouts, signs_number(): r2 = jnp.concatenate(newest, axis=2)  2.61 us
    all_gather x1, blocking collectives, per_device(): spectra = lax.all_gather(half_spec, 'cmp', axis=1, tiled=True)  2.59 us
  transfers between devices with their start and end apart: 2, of which 1 were waited for; matrix products, arithmetic and copies ran while one was open for 12% of the time, Pallas kernels for 0%

profile of v1, /device:TPU:0, one launch (start us, length us, event | category | flops | bytes accessed | tf_op | source)
XLA Modules:
  0.0 113.3 jit_solution(14642150213830420238)
XLA Ops:
  6.6 0.8 and_select_fusion
  7.4 0.2 convert_reduce_fusion
  7.8 0.7 scatter_custom_fusion.1
  8.5 3.9 %gather_fusion.5 = bf16[16,3,3,4096]{3,0,2,1:T(8,128)(2,1)S(1)} fusion(bf16[3,3,16,4096]{3,2,1,0:T(8,128)(2,1)S(1)} %copy-done, s32[1024]{0:T(1024)S(1)} %pad_clamp_fusion.1), kind=kCustom, calls=%fused_computation.5 | custom fusion | bytes 2359360 | tf_op jit(solution)/shard_map/jit(_take)/gather | solution.py:118
  12.5 0.7 scatter_custom_fusion
  13.1 0.2 select_bitcast_fusion
  13.3 0.6 slice_bitcast_fusion.3
  13.9 2.1 %pad_maximum_fusion = bf16[4,3,3,4,4096]{4,3,2,1,0:T(4,128)(2,1)} fusion(bf16[1,3,3,4,4096]{4,3,2,1,0:T(4,128)(2,1)S(1)} %get-tuple-element.17, bf16[1,3,3,4,4096]{4,3,2,1,0:T(4,128)(2,1)S(1)} %get-tuple-element.18, bf16[1,3,3,4,4096]{4,3,2,1,0:T(4,128)(2,1)S(1)} %get-tuple-element.19, bf16[1,3,3,4,4096]{4,3,2,1,0:T(4,128)(2,1)S(1)} %get-tuple-element.16), kind=kLoop, calls=%fused_computation.12 | loop fusion | flops 1769472 | bytes 2359296 | tf_op jit(solution)/shard_map/stack | solution.py:15
  16.0 6.5 %all-to-all-start = ((bf16[4,3,3,4,4096]{4,3,2,1,0:T(4,128)(2,1)}), bf16[4,3,3,4,4096]{4,3,2,1,0:T(4,128)(2,1)S(1)}, u32[]{:S(2)}, u32[]{:S(2)}) async-start(bf16[4,3,3,4,4096]{4,3,2,1,0:T(4,128)(2,1)} %pad_maximum_fusion), calls=%async_computation | async-start | bytes 2359296 | tf_op jit(solution)/shard_map/all_to_all | solution.py:16
  22.5 0.7 sine_negate_fusion
  23.2 0.6 compare_and_fusion.3
  23.8 0.6 pad_clamp_fusion
  24.4 0.7 copy.52
  25.1 22.5 %all-gather = s32[4,1,6]{2,1,0:T(1,128)S(1)} all-gather(s32[1,1,6]{2,1,0:T(1,128)S(1)} %bitcast.114), channel_id=1, replica_groups=mesh['site'=2,'pts'=4,'var'=2,'cmp'=2] {'pts'}, dimensions={0}, use_global_device_ids=true | all-gather | bytes 120 | tf_op jit(solution)/shard_map/all_gather | solution.py:131
  48.0 0.6 gather_fusion
  48.7 0.6 gather_fusion.3
  49.4 0.6 gather_fusion.1
  50.0 1.7 %gather_fusion.2 = f32[4,2,4096]{2,1,0:T(2,128)S(1)} fusion(f32[16,2,4096]{2,1,0:T(2,128)} %param.10, s32[1024]{0:T(1024)S(1)} %pad_clamp_fusion.3), kind=kCustom, calls=%fused_computation.2 | custom fusion | bytes 262160 | tf_op jit(solution)/shard_map/gather | solution.py:179
  51.8 0.2 reshape.317
  52.2 0.6 gather_fusion.4
  52.9 0.2 select_reduce_fusion
  53.1 0.3 copy-done.9
  53.7 0.3 fusion.61
  54.0 0.9 fusion.54
  54.9 0.6 iota_add_fusion.1
  55.5 0.6 broadcast_multiply_fusion.1
  56.1 1.2 %fusion.48 = (f32[4,64,64]{2,0,1:T(4,128)S(1)}, f32[4,64,64]{2,0,1:T(4,128)S(1)}) fusion(s32[4]{0:T(128)S(1)} %get-tuple-element.8, s32[64,64]{1,0:T(8,128)S(1)} %iota_add_fusion), kind=kLoop, calls=%fused_computation.94 | loop fusion | flops 229376 | bytes 147472 | tf_op jit(solution)/shard_map/cos | solution.py:26
  57.3 1.1 fusion.41
  58.4 2.6 %copy.67 = bf16[3,3,4,4,4096]{4,1,3,2,0:T(4,128)(2,1)} copy(bf16[3,3,4,4,4096]{4,3,1,0,2:T(4,128)(2,1)S(1)} %bitcast.100) | data formatting | bytes 2359296 | tf_op jit(solution)/shard_map/reshape | solution.py:17
  61.0 2.7 %gather_fusion.6 = bf16[8,3,3,4096]{3,2,1,0:T(4,128)(2,1)S(1)} fusion(bf16[3,3,16,4096]{3,1,2,0:T(4,128)(2,1)} %bitcast.101, s32[1024]{0:T(1024)} %pad_clamp_fusion), kind=kCustom, calls=%fused_computation.6 | custom fusion | bytes 1179680 | tf_op jit(solution)/shard_map/jit(_take)/gather | solution.py:122
  63.8 0.7 fusion
  64.5 0.4 copy.55
  64.9 4.0 %all_to_all.17 = f32[1,3,8,4096]{3,0,1,2:T(1,128)S(1)} all-to-all(f32[1,3,8,4096]{3,0,1,2:T(1,128)S(1)} %copy.55), channel_id=1, replica_groups=mesh['site'=2,'pts'=4,'var'=2,'cmp'=2] {'cmp'}, dimensions={2} | all-to-all | bytes 786432 | tf_op jit(solution)/shard_map/all_to_all | solution.py:124
  69.0 0.3 copy.70
  69.2 0.2 reduce_sum.82
  69.7 0.9 convolution_bitcast_fusion
  70.8 0.9 fusion.1
  71.7 2.6 %all_gather.7 = f32[3,8,64,128]{3,2,0,1:T(8,128)S(1)} all-gather(f32[3,4,64,128]{3,2,0,1:T(8,128)S(1)} %copy.59), channel_id=1, replica_groups=mesh['site'=2,'pts'=4,'var'=2,'cmp'=2] {'cmp'}, dimensions={1}, use_global_device_ids=true | all-gather | bytes 1179648 | tf_op jit(solution)/shard_map/all_gather | solution.py:130
  74.3 0.3 fusion.114
  74.6 1.0 fusion.14
  75.6 0.6 fusion.5
  76.3 0.6 fusion.9
  76.9 0.5 multiply_subtract_fusion
  77.5 0.3 pad_maximum_fusion.1
  77.8 0.8 copy.62
  79.1 25.3 %reduce-scatter.2.cloned.1.call-done = f32[1,3,64,128]{3,2,1,0:T(8,128)} async-done(((f32[4,3,64,128]{3,2,1,0:T(8,128)}), f32[1,3,64,128]{3,2,1,0:T(8,128)}) %reduce-scatter.2.cloned.1.call-update) | async-done | bytes 98320 | tf_op jit(solution)/shard_map/reduce_scatter | solution.py:194
  104.3 1.2 %fusion.33 = f32[3,64,256]{2,1,0:T(8,128)S(1)} fusion(f32[64,128]{1,0:T(8,128)S(1)} %get-tuple-element.47, f32[64,128]{1,0:T(8,128)S(1)} %get-tuple-element.48, f32[64,128]{1,0:T(8,128)S(1)} %get-tuple-element.46, f32[1,3,64,128]{3,2,1,0:T(8,128)} %reduce-scatter.2.cloned.1.call-done, f32[64,128]{1,0:T(8,128)S(1)} %get-tuple-element.45), kind=kOutput, calls=%fused_computation.73 | convolution fusion | flops 75620352 | bytes 425984 | tf_op jit(solution)/shard_map/skm,mb->skb/dot_general | solution.py:80
  105.6 0.9 fusion.20
  (80 shorter events, 2.3 us)
Async XLA Ops:
  6.5 2.0 %copy-start = (bf16[3,3,16,4096]{3,2,1,0:T(8,128)(2,1)S(1)}, bf16[3,3,16,4096]{3,2,1,0:T(8,128)(2,1)}, u32[]{:S(2)}) copy-start(bf16[3,3,16,4096]{3,2,1,0:T(8,128)(2,1)} %param.8) | copy-start | bytes 3538948
  16.0 8.4 %copy-start.17 = (f32[3,8]{1,0:T(4,128)S(1)}, f32[3,8]{1,0:T(4,128)}, u32[]{:S(2)}) copy-start(f32[3,8]{1,0:T(4,128)} %param.9) | copy-start | bytes 292
  16.0 9.1 %copy-start.18 = (s32[1,6]{1,0:T(1,128)S(1)}, s32[1,6]{1,0:T(1,128)}, u32[]{:S(2)}) copy-start(s32[1,6]{1,0:T(1,128)} %param.12) | copy-start | bytes 76
  16.0 32.0 %copy-start.2 = (s32[16]{0:T(128)S(1)}, s32[16]{0:T(128)}, u32[]{:S(2)}) copy-start(s32[16]{0:T(128)} %param.15) | copy-start | bytes 196
  16.0 32.7 %copy-start.1 = (s32[16,2]{0,1:T(2,128)S(1)}, s32[16,2]{0,1:T(2,128)}, u32[]{:S(2)}) copy-start(s32[16,2]{0,1:T(2,128)} %param.14) | copy-start | bytes 388
  16.0 42.3 %all-to-all-start = ((bf16[4,3,3,4,4096]{4,3,2,1,0:T(4,128)(2,1)}), bf16[4,3,3,4,4096]{4,3,2,1,0:T(4,128)(2,1)S(1)}, u32[]{:S(2)}, u32[]{:S(2)}) async-start(bf16[4,3,3,4,4096]{4,3,2,1,0:T(4,128)(2,1)} %pad_maximum_fusion), calls=%async_computation | async-start | bytes 2359296 | tf_op jit(solution)/shard_map/all_to_all | solution.py:16
  22.5 81.8 %reduce-scatter.2.cloned.1.call-start = ((), (), s32[]{:S(2)}) async-start(), calls=%async_computation.3 | async-start | bytes 491520 | tf_op jit(solution)/shard_map/reduce_scatter | solution.py:194
  48.0 4.9 %copy-start.11 = (s32[8]{0:T(128)}, s32[8]{0:T(128)S(1)}, u32[]{:S(2)}) copy-start(s32[8]{0:T(128)S(1)} %convert_reduce_fusion.1) | copy-start | bytes 100
  49.4 2.9 %copy-start.3 = (s32[16]{0:T(128)S(1)}, s32[16]{0:T(128)}, u32[]{:S(2)}) copy-start(s32[16]{0:T(128)} %param.13) | copy-start | bytes 196
  52.9 0.5 copy-start.9
  52.9 3.2 %copy-start.13 = (s32[64]{0:T(128)}, s32[64]{0:T(128)S(1)}, u32[]{:S(2)}) copy-start(s32[64]{0:T(128)S(1)} %iota_multiply_fusion.2) | copy-start | bytes 772
  61.0 2.8 %copy-start.7 = (f32[3,8]{0,1:T(8,128)S(1)}, f32[3,8]{0,1:T(8,128)}, u32[]{:S(2)}) copy-start(f32[3,8]{0,1:T(8,128)} %copy.52) | copy-start | bytes 292
  61.0 2.8 %copy-start.16 = (pred[8]{0:T(512)(128)(4,1)S(1)}, pred[8]{0:T(512)(128)(4,1)}, u32[]{:S(2)}) copy-start(pred[8]{0:T(512)(128)(4,1)} %get-tuple-element.10) | copy-start | bytes 28
  69.0 0.8 copy-start.6
  69.7 1.0 copy-start.4
  69.7 1.0 copy-start.5
  74.6 1.1 copy-start.8
  74.6 1.1 copy-start.10
  74.6 1.1 copy-start.12
  74.6 1.1 copy-start.15
  77.5 1.4 %copy-start.14 = (s32[64]{0:T(128)S(1)}, s32[64]{0:T(128)}, u32[]{:S(2)}) copy-start(s32[64]{0:T(128)} %copy-done.13) | copy-start | bytes 772
Sparse Core Ops, SparseCore 0:
  78.8 25.5 reduce-scatter.1
